TPU v7x, 32 devices: a whole 2x2x4 slice. The times are simulated.
32 devices in a mesh: gx: 8 (over z, y), gy: 4 (over x, core).
Axes of the slice: x: 2, y: 2, z: 4, core: 2. Of those that a mesh axis runs over, the one named last changes fastest.
Arguments:
- coarse_send: bfloat16 [8, 35, 4096], P('gx', None, 'gy'), may hold values from -6 to 6
- coarse_flux: float32 [8, 35, 1024], P('gx', None, 'gy'), may hold values from -6 to 6
- patch_owner: int32 [8], replicated, may hold values from 0 to 15, as said below
- velocity: float32 [3], replicated, may hold values from -0.6 to 0.6
- diffusivity: float32 [35], replicated, may hold values from 0.03 to 0.15
- stoich: float32 [35, 35], replicated, may hold values from -1 to 1
Outputs:
- fine_state: float32 [16, 35, 32768], P('gx', None, 'gy')
- reflux: float32 [8, 35, 1024], P('gx', None, 'gy')
Inputs may be any that keep to these rules, and one draw needn't show every extreme that they name: `patch_owner`: the 8 entries are distinct; slot s belongs to owner group s // 2, the group of index s // 2 along gx; a group owns 0, 1 or 2 patches, and at least one group owns exactly 2.
All inputs are finite; a program needn't handle non-finite values.
Results may differ from a plain program's by a relative error of at most 0.0003.
Values may be sent and summed in bfloat16 or wider, within the bound.
No kernel may reach another device: no remote copies, remote signals or barrier semaphores. Data moves between devices by JAX's collectives and lax.ppermute only.
A program may use at most 128 MiB of HBM per device.

v0:
```python
import jax
import jax.numpy as jnp
from jax import lax
from jax.sharding import PartitionSpec as P

CB = 16
time_step = 0.25
heat_gain = 2.0
highest = lax.Precision.HIGHEST


def padded(block, sides, width):
    for axis, dim in sides:
        count = lax.axis_size(axis)
        forward = [(i, i + 1) for i in range(count - 1)]
        backward = [(target, source) for source, target in forward]
        low = lax.ppermute(
            lax.slice_in_dim(block, block.shape[dim] - width, None, axis=dim), axis, forward
        )
        high = lax.ppermute(lax.slice_in_dim(block, 0, width, axis=dim), axis, backward)
        block = jnp.concatenate([low, block, high], axis=dim)
    return block


def axis_slope(values, axis):
    moved = jnp.moveaxis(values, axis, 0)
    middle = (moved[2:] - moved[:-2]) * 0.5
    joined = jnp.concatenate([moved[1:2] - moved[0:1], middle, moved[-1:] - moved[-2:-1]], 0)
    return jnp.moveaxis(joined, 0, axis)


def spread(values):
    return values[..., :, None, :, None, :, None]


def refine(coarse, slope_z, slope_y, slope_x):
    offsets = jnp.array([-0.5, 0.5], jnp.float32)
    leading = coarse.shape[:-3]
    depth, height, breadth = coarse.shape[-3:]
    shift_y = offsets[:, None, None]
    shift_z = offsets[:, None, None, None, None]
    terms = spread(slope_x) * offsets + spread(slope_y) * shift_y + spread(slope_z) * shift_z
    fine_cells = spread(coarse) + terms * 0.5
    return fine_cells.reshape(leading + (2 * depth, 2 * height, 2 * breadth))


def face_flux(left_side, right_side, speed, diffuse):
    return speed * (left_side + right_side) * 0.5 - diffuse * (right_side - left_side)


def tendency(padded_layers, cells, velocity, diffusivity, stoich):
    diffuse = diffusivity[:, None, None, None]
    padded_cols = jnp.concatenate([cells[..., :1], cells, cells[..., -1:]], -1)
    padded_rows = jnp.concatenate([cells[..., :1, :], cells, cells[..., -1:, :]], -2)
    flux_cols = face_flux(padded_cols[..., :-1], padded_cols[..., 1:], velocity[0], diffuse)
    flux_rows = face_flux(padded_rows[..., :-1, :], padded_rows[..., 1:, :], velocity[1], diffuse)
    flux_layers = face_flux(
        padded_layers[..., :-1, :, :], padded_layers[..., 1:, :, :], velocity[2], diffuse
    )
    outflow = (
        flux_cols[..., 1:]
        - flux_cols[..., :-1]
        + (flux_rows[..., 1:, :] - flux_rows[..., :-1, :])
        + (flux_layers[..., 1:, :, :] - flux_layers[..., :-1, :, :])
    )
    reaction_rate = cells * jax.nn.sigmoid(heat_gain * cells[..., 0:1, :, :, :])
    source = jnp.einsum("fg,...gzyx->...fzyx", stoich, reaction_rate, precision=highest)
    side_fluxes = (
        flux_cols[..., 0],
        flux_cols[..., -1],
        flux_rows[..., 0, :],
        flux_rows[..., -1, :],
    )
    return (source - outflow, side_fluxes)


def tendency_slots(padded_layers, cells, velocity, diffusivity, stoich):

    def tendency_one_slot(pair):
        return tendency(pair[0], pair[1], velocity, diffusivity, stoich)

    return lax.map(tendency_one_slot, (padded_layers, cells))


def refine_slots(coarse, slope_z):

    def refine_one_slot(pair):
        block, slope_layers = pair
        return refine(block, slope_layers, axis_slope(block, 2), axis_slope(block, 3))

    return lax.map(refine_one_slot, (coarse, slope_z))


def average_sides(earlier, later_sides):
    return jnp.stack(
        [
            (earlier[0] + later_sides[0]) * 0.5,
            (earlier[1] + later_sides[1]) * 0.5,
            (earlier[2] + later_sides[2]) * 0.5,
            (earlier[3] + later_sides[3]) * 0.5,
        ],
        -2,
    )


def coarsen_faces(register):
    leading = register.shape[:-3]
    depth = register.shape[-3] // 2
    along = register.shape[-1] // 2
    split_faces = register.reshape(leading + (depth, 2, 4, along, 2))
    return (
        split_faces[..., 0, :, :, 0]
        + split_faces[..., 0, :, :, 1]
        + split_faces[..., 1, :, :, 0]
        + split_faces[..., 1, :, :, 1]
    ) * 0.25


def route_home(values, patch_owner, my_slots):
    chooser = (patch_owner[:, None] == my_slots[None, :]).astype(jnp.float32)
    return jnp.einsum("qo,ofc->qfc", chooser, values, precision=highest)


def shards(coarse_send, coarse_flux, patch_owner, velocity, diffusivity, stoich):
    send_slots, fields, layer_cells = coarse_send.shape
    own_slots = 2 * send_slots
    owner_group = lax.axis_index("gx")
    pencil = lax.axis_index("gy")
    pencils = lax.axis_size("gy")
    block_edge = CB
    layers = layer_cells // (block_edge * block_edge)
    my_slots = owner_group * own_slots + jnp.arange(own_slots, dtype=jnp.int32)
    chooser = (my_slots[:, None] == patch_owner[None, :]).astype(jnp.bfloat16)
    gathered = jnp.einsum(
        "oq,qfc->ofc",
        chooser,
        lax.all_gather(coarse_send, "gx", axis=0, tiled=True),
        preferred_element_type=jnp.float32,
    )
    coarse = gathered.reshape(own_slots, fields, layers, block_edge, block_edge)
    rimmed = padded(coarse.astype(jnp.bfloat16), (("gy", 2),), 1).astype(coarse.dtype)
    below = rimmed[:, :, :-2]
    above = rimmed[:, :, 2:]
    depth_index = pencil * layers + jnp.arange(layers, dtype=jnp.int32)
    is_first = (depth_index == 0)[:, None, None]
    is_last = (depth_index == block_edge - 1)[:, None, None]
    slope_z = jnp.where(
        is_first, above - coarse, jnp.where(is_last, coarse - below, (above - below) * 0.5)
    )
    fine_cells = refine_slots(coarse, slope_z)
    at_bottom = pencil == 0
    at_top = pencil == pencils - 1

    def extend_layers(cells):
        ghosts = padded(cells.astype(jnp.bfloat16), (("gy", 2),), 1).astype(cells.dtype)
        lower_ghost = jnp.where(at_bottom, cells[:, :, :1], ghosts[:, :, :1])
        upper_ghost = jnp.where(at_top, cells[:, :, -1:], ghosts[:, :, -1:])
        return jnp.concatenate([lower_ghost, cells, upper_ghost], 2)

    change, first_sides = tendency_slots(
        extend_layers(fine_cells), fine_cells, velocity, diffusivity, stoich
    )
    section_state = fine_cells + time_step * change
    second, second_sides = tendency_slots(
        extend_layers(section_state), section_state, velocity, diffusivity, stoich
    )
    final_state = fine_cells + time_step * 0.5 * (change + second)
    register = average_sides(first_sides, second_sides)
    flat_faces = coarsen_faces(register).reshape(own_slots, fields, -1)
    summed = lax.psum_scatter(
        route_home(flat_faces, patch_owner, my_slots), "gx", scatter_dimension=0, tiled=True
    )
    averaged = summed.reshape(send_slots, fields, layers, 4, block_edge)
    corrected = averaged - coarse_flux.reshape(send_slots, fields, layers, 4, block_edge)
    return (final_state.reshape(own_slots, fields, -1), corrected.reshape(send_slots, fields, -1))


def solution(mesh):
    placed = (P("gx", None, "gy"), P("gx", None, "gy"), P(), P(), P(), P())
    return jax.shard_map(
        shards,
        mesh=mesh,
        in_specs=placed,
        out_specs=(P("gx", None, "gy"), P("gx", None, "gy")),
        check_vma=False,
    )
```

profile of v0, /device:TPU:0, one launch (start us, length us, event | category | flops | bytes accessed | tf_op | source)
XLA Modules:
  0.0 392.6 jit_solution(8805554592416697023)
XLA Ops:
  7.2 33.6 %all_gather.3 = bf16[8,35,1024]{2,1,0:T(8,128)(2,1)S(1)} all-gather(bf16[1,35,1024]{2,1,0:T(8,128)(2,1)} %param.13), channel_id=1, replica_groups=mesh['gx'=8,'gy'=4] {'gx'}, dimensions={0}, use_global_device_ids=true | all-gather | bytes 645120 | tf_op jit(solution)/shard_map/all_gather | solution.py:137
  49.3 4.5 %broadcast.182.clone = f32[2,35,8,32,32]{1,4,3,2,0:T(8,128)} broadcast(f32[]{:T(128)} %constant.54.clone.1), dimensions={} | broadcast | bytes 2293764 | tf_op jit(solution)/shard_map/broadcast.31
  53.8 17.1 %while.49 = (s32[]{:T(128)}, f32[2,35,8,32,32]{1,4,3,2,0:T(8,128)}, f32[2,35,4,16,16]{1,4,3,2,0:T(8,128)S(1)}, f32[2,35,4,16,16]{1,4,3,2,0:T(8,128)S(1)}, s32[]{:T(128)}, /*index=5*/f32[2]{0:T(128)S(1)}) while((s32[]{:T(128)}, f32[2,35,8,32,32]{1,4,3,2,0:T(8,128)}, f32[2,35,4,16,16]{1,4,3,2,0:T(8,128)S(1)}, ...), condition=%wide.region_1.2_spmd.clone, body=%wide.region_0.1_spmd.sunk.clone.sunk | while | flops 1496322 | bytes 12653153 | solution.py:91
  70.9 4.5 %convert_element_type.22 = bf16[2,35,8,32,32]{1,4,3,2,0:T(8,128)(2,1)S(1)} convert(f32[2,35,8,32,32]{1,4,3,2,0:T(8,128)} %get-tuple-element.589) | non-fusion elementwise | flops 573440 | bytes 3440640 | tf_op jit(solution)/shard_map/convert_element_type | solution.py:155
  77.5 5.5 %collective-permute-start.2 = (bf16[2,35,1,32,32]{1,4,3,2,0:T(8,128)(2,1)S(1)}, bf16[2,35,1,32,32]{1,4,3,2,0:T(8,128)(2,1)S(1)}, u32[]{:S(2)}, u32[]{:S(2)}) collective-permute-start(bf16[2,35,1,32,32]{1,4,3,2,0:T(8,128)(2,1)S(1)} %get-tuple-element.338), channel_id=1, source_target_pairs={{0,1},{1,2},{2,3},{4,5},{5,6},{6,7},{8,9},{9,10},{10,11},{12,13},{... | collective-permute-start | bytes 430088 | tf_op jit(solution)/shard_map/ppermute | solution.py:17
  88.7 9.3 %pad_maximum_fusion.8 = f32[2,35,10,32,32]{1,4,3,2,0:T(8,128)} fusion(f32[2,35,1,32,32]{1,4,3,2,0:T(8,128)S(1)} %get-tuple-element.335, f32[2,35,8,32,32]{1,4,3,2,0:T(8,128)} %get-tuple-element.589, f32[2,35,1,32,32]{1,4,3,2,0:T(8,128)S(1)} %get-tuple-element.334), kind=kLoop, calls=%fused_computation.78 | loop fusion | flops 1433600 | bytes 5734400 | tf_op jit(solution)/shard_map/concatenate | solution.py:158
  102.5 81.6 %while.47 = (s32[]{:T(128)}, f32[2,35,8,32,32]{1,4,3,2,0:T(8,128)}, f32[2,35,8,32]{1,3,2,0:T(8,128)S(1)}, f32[2,35,8,32]{1,3,2,0:T(8,128)S(1)}, f32[2,35,8,32]{1...) while((s32[]{:T(128)}, f32[2,35,8,32,32]{1,4,3,2,0:T(8,128)}, ...), condition=%wide.region_3.4_spmd, body=%wide.region_2.3_spmd.sunk | while | flops 129128448 | bytes 80370104 | solution.py:82
  106.5 4.4 %multiply_subtract_fusion.14 = f32[35,8,32,33]{0,3,2,1:T(8,128)} fusion(f32[35,8,32,1]{0,3,2,1:T(1,128)S(1)} %get-tuple-element.523, f32[35,8,32,32]{0,3,2,1:T(8,128)S(1)} %dynamic-slice_bitcast_fusion.15, f32[35,8,32,1]{0,3,2,1:T(1,128)S(1)} %get-tuple-element.524, f32[35]{0:T(128)S(1)} %get-tuple-element.616, f32[]{:T(128)} %bitcast.137), kind=kLoop, calls=%fused_computation.3.clone.1 | loop fusion | flops 2365440 | bytes 2401424 | tf_op jit(solution)/shard_map/while/body/eval_jaxpr/sub | solution.py:48
  118.7 4.6 %constant_dynamic-slice_fusion.4 = f32[1,1,8,32,32]{1,4,3,2,0:T(8,128)} fusion(f32[2,35,8,32,32]{1,4,3,2,0:T(8,128)} %get-tuple-element.613, s32[]{:T(128)} %get-tuple-element.595), kind=kLoop, calls=%fused_computation.26.clone.1 | loop fusion | bytes 65540 | tf_op jit(solution)/shard_map/while/body/eval_jaxpr/slice | solution.py:66
  126.5 14.0 %fusion.78 = f32[2,35,8,32,32]{1,4,3,2,0:T(8,128)} fusion(f32[2,35,8,32,32]{1,4,3,2,0:T(8,128)} %get-tuple-element.596, s32[]{:T(128)} %get-tuple-element.595, f32[35,9,32,32]{0,3,2,1:T(8,128)} %multiply_subtract_fusion.12, f32[35,8,33,32]{0,3,2,1:T(8,128)} %multiply_subtract_fusion.13, f32[35,8,32,33]{0,3,2,1:T(8,128)} %multiply_subtract_fusion.14, ...), kind=kOutput, calls=%fused_computation.12.clone.1 | convolution fusion | flops 122429440 | bytes 33593124 | tf_op jit(solution)/shard_map/while/body/eval_jaxpr/fg,...gzyx->...fzyx/dot_general | solution.py:67
  159.3 4.6 %constant_dynamic-slice_fusion.4 = f32[1,1,8,32,32]{1,4,3,2,0:T(8,128)} fusion(f32[2,35,8,32,32]{1,4,3,2,0:T(8,128)} %get-tuple-element.613, s32[]{:T(128)} %get-tuple-element.595), kind=kLoop, calls=%fused_computation.26.clone.1 | loop fusion | bytes 65540 | tf_op jit(solution)/shard_map/while/body/eval_jaxpr/slice | solution.py:66
  167.2 14.1 %fusion.78 = f32[2,35,8,32,32]{1,4,3,2,0:T(8,128)} fusion(f32[2,35,8,32,32]{1,4,3,2,0:T(8,128)} %get-tuple-element.596, s32[]{:T(128)} %get-tuple-element.595, f32[35,9,32,32]{0,3,2,1:T(8,128)} %multiply_subtract_fusion.12, f32[35,8,33,32]{0,3,2,1:T(8,128)} %multiply_subtract_fusion.13, f32[35,8,32,33]{0,3,2,1:T(8,128)} %multiply_subtract_fusion.14, ...), kind=kOutput, calls=%fused_computation.12.clone.1 | convolution fusion | flops 122429440 | bytes 33593124 | tf_op jit(solution)/shard_map/while/body/eval_jaxpr/fg,...gzyx->...fzyx/dot_general | solution.py:67
  184.0 12.9 %fusion.42 = (bf16[2,35,8,32,32]{1,4,3,2,0:T(8,128)(2,1)}, f32[2,35,8,32,32]{1,4,3,2,0:T(8,128)}) fusion(f32[2,35,8,32,32]{1,4,3,2,0:T(8,128)} %get-tuple-element.589, f32[2,35,8,32,32]{1,4,3,2,0:T(8,128)} %get-tuple-element.152), kind=kLoop, calls=%fused_computation.120 | loop fusion | flops 1720320 | bytes 8028160 | tf_op jit(solution)/shard_map/convert_element_type | solution.py:155
  199.0 8.6 %collective-permute-start.4 = (bf16[2,35,1,32,32]{1,4,3,2,0:T(8,128)(2,1)}, bf16[2,35,1,32,32]{1,4,3,2,0:T(8,128)(2,1)S(1)}, u32[]{:S(2)}, u32[]{:S(2)}) collective-permute-start(bf16[2,35,1,32,32]{1,4,3,2,0:T(8,128)(2,1)} %get-tuple-element.336), channel_id=1, source_target_pairs={{0,1},{1,2},{2,3},{4,5},{5,6},{6,7},{8,9},{9,10},{10,11},{12,13},{... | collective-permute-start | bytes 430088 | tf_op jit(solution)/shard_map/ppermute | solution.py:17
  215.5 5.8 %pad_maximum_fusion.9 = f32[2,35,10,32,32]{1,4,3,2,0:T(8,128)} fusion(f32[2,35,1,32,32]{1,4,3,2,0:T(8,128)S(1)} %get-tuple-element.333, f32[2,35,8,32,32]{1,4,3,2,0:T(8,128)S(1)} %copy-done, f32[2,35,1,32,32]{1,4,3,2,0:T(8,128)S(1)} %get-tuple-element.332), kind=kLoop, calls=%fused_computation.79 | loop fusion | flops 1433600 | bytes 5734400 | tf_op jit(solution)/shard_map/concatenate | solution.py:158
  221.3 4.4 %broadcast.182 = f32[2,35,8,32,32]{1,4,3,2,0:T(8,128)} broadcast(f32[]{:T(128)} %constant.54.clone.1), dimensions={} | broadcast | bytes 2293764 | tf_op jit(solution)/shard_map/broadcast.31
  225.8 78.0 %while.48 = (s32[]{:T(128)}, f32[2,35,8,32,32]{1,4,3,2,0:T(8,128)}, f32[2,35,8,32]{1,3,2,0:T(8,128)S(1)}, f32[2,35,8,32]{1,3,2,0:T(8,128)S(1)}, f32[2,35,8,32]{1...) while((s32[]{:T(128)}, f32[2,35,8,32,32]{1,4,3,2,0:T(8,128)}, ...), condition=%wide.region_5.6_spmd, body=%wide.region_4.5_spmd.sunk | while | flops 129128448 | bytes 105535960 | solution.py:82
  229.8 4.4 %multiply_subtract_fusion.17 = f32[35,8,32,33]{0,3,2,1:T(8,128)} fusion(f32[35,8,32,1]{0,3,2,1:T(1,128)S(1)} %get-tuple-element.546, f32[35,8,32,32]{0,3,2,1:T(8,128)S(1)} %dynamic-slice_bitcast_fusion.17, f32[35,8,32,1]{0,3,2,1:T(1,128)S(1)} %get-tuple-element.547, f32[35]{0:T(128)S(1)} %get-tuple-element.652, f32[]{:T(128)} %bitcast.150), kind=kLoop, calls=%fused_computation.32.clone.1 | loop fusion | flops 2365440 | bytes 2401424 | tf_op jit(solution)/shard_map/while/body/eval_jaxpr/sub | solution.py:48
  248.1 14.1 %fusion.86 = f32[2,35,8,32,32]{1,4,3,2,0:T(8,128)} fusion(f32[2,35,8,32,32]{1,4,3,2,0:T(8,128)} %get-tuple-element.632, s32[]{:T(128)} %get-tuple-element.631, f32[35,9,32,32]{0,3,2,1:T(8,128)} %multiply_subtract_fusion.15, f32[35,8,33,32]{0,3,2,1:T(8,128)} %multiply_subtract_fusion.16, f32[35,8,32,33]{0,3,2,1:T(8,128)} %multiply_subtract_fusion.17, ...), kind=kOutput, calls=%fused_computation.41.clone.1 | convolution fusion | flops 122429440 | bytes 33593124 | tf_op jit(solution)/shard_map/while/body/eval_jaxpr/fg,...gzyx->...fzyx/dot_general | solution.py:67
  268.7 4.4 %multiply_subtract_fusion.17 = f32[35,8,32,33]{0,3,2,1:T(8,128)} fusion(f32[35,8,32,1]{0,3,2,1:T(1,128)S(1)} %get-tuple-element.546, f32[35,8,32,32]{0,3,2,1:T(8,128)S(1)} %dynamic-slice_bitcast_fusion.17, f32[35,8,32,1]{0,3,2,1:T(1,128)S(1)} %get-tuple-element.547, f32[35]{0:T(128)S(1)} %get-tuple-element.652, f32[]{:T(128)} %bitcast.150), kind=kLoop, calls=%fused_computation.32.clone.1 | loop fusion | flops 2365440 | bytes 2401424 | tf_op jit(solution)/shard_map/while/body/eval_jaxpr/sub | solution.py:48
  287.0 14.1 %fusion.86 = f32[2,35,8,32,32]{1,4,3,2,0:T(8,128)} fusion(f32[2,35,8,32,32]{1,4,3,2,0:T(8,128)} %get-tuple-element.632, s32[]{:T(128)} %get-tuple-element.631, f32[35,9,32,32]{0,3,2,1:T(8,128)} %multiply_subtract_fusion.15, f32[35,8,33,32]{0,3,2,1:T(8,128)} %multiply_subtract_fusion.16, f32[35,8,32,33]{0,3,2,1:T(8,128)} %multiply_subtract_fusion.17, ...), kind=kOutput, calls=%fused_computation.41.clone.1 | convolution fusion | flops 122429440 | bytes 33593124 | tf_op jit(solution)/shard_map/while/body/eval_jaxpr/fg,...gzyx->...fzyx/dot_general | solution.py:67
  305.6 13.3 %multiply_add_fusion.1 = f32[2,35,8,32,32]{1,4,3,2,0:T(8,128)} fusion(f32[2,35,8,32,32]{1,4,3,2,0:T(8,128)} %get-tuple-element.589, f32[2,35,8,32,32]{1,4,3,2,0:T(8,128)} %get-tuple-element.152, f32[2,35,8,32,32]{1,4,3,2,0:T(8,128)} %get-tuple-element.153), kind=kLoop, calls=%fused_computation.80 | loop fusion | flops 1720320 | bytes 9175040 | tf_op jit(solution)/shard_map/add | solution.py:167
  319.0 7.2 %copy.61 = f32[2,35,8192]{2,0,1:T(2,128)} copy(f32[2,35,8192]{1,2,0:T(8,128)} %bitcast.167) | data formatting | bytes 4587520 | tf_op jit(solution)/shard_map/reshape | solution.py:175
  326.2 57.2 %all-reduce.3.cloned.1.call-done = f32[8,35,256]{2,0,1:T(8,128)} async-done(((f32[8,35,256]{2,0,1:T(8,128)}), f32[8,35,256]{2,0,1:T(8,128)}) %all-reduce.3.cloned.1.call-update) | async-done | bytes 286736
  (187 shorter events, 131.6 us)
Async XLA Ops:
  7.2 376.2 %all-reduce.3.cloned.1.call-start = ((), (), s32[]{:S(2)}) async-start(), calls=%async_computation | async-start | bytes 573440
  7.2 33.6 %copy-start.8 = (s32[2]{0:T(128)}, s32[2]{0:T(128)S(1)}, u32[]{:S(2)}) copy-start(s32[2]{0:T(128)S(1)} %iota_add_fusion.1) | copy-start | bytes 28
  42.5 2.6 collective-permute-start
  43.8 5.0 %collective-permute-start.1 = (bf16[2,35,1,16,16]{1,4,3,2,0:T(8,128)(2,1)S(1)}, bf16[2,35,1,16,16]{1,4,3,2,0:T(8,128)(2,1)S(1)}, u32[]{:S(2)}, u32[]{:S(2)}) collective-permute-start(bf16[2,35,1,16,16]{1,4,3,2,0:T(8,128)(2,1)S(1)} %get-tuple-element.341), channel_id=1, source_target_pairs={{1,0},{2,1},{3,2},{5,4},{6,5},{7,6},{9,8},{10,9},{11,10},{13,12},{... | collective-permute-start | bytes 107528 | tf_op jit(solution)/shard_map/ppermute | solution.py:20
  49.3 4.5 %copy-start.5 = (f32[2]{0:T(128)S(1)}, f32[2]{0:T(128)}, u32[]{:S(2)}) copy-start(f32[2]{0:T(128)} %constant.89.clone..sunk.2) | copy-start | bytes 28
  77.5 7.0 %collective-permute-start.2 = (bf16[2,35,1,32,32]{1,4,3,2,0:T(8,128)(2,1)S(1)}, bf16[2,35,1,32,32]{1,4,3,2,0:T(8,128)(2,1)S(1)}, u32[]{:S(2)}, u32[]{:S(2)}) collective-permute-start(bf16[2,35,1,32,32]{1,4,3,2,0:T(8,128)(2,1)S(1)} %get-tuple-element.338), channel_id=1, source_target_pairs={{0,1},{1,2},{2,3},{4,5},{5,6},{6,7},{8,9},{9,10},{10,11},{12,13},{... | collective-permute-start | bytes 430088 | tf_op jit(solution)/shard_map/ppermute | solution.py:17
  83.0 3.8 collective-permute-start.3
  97.9 4.5 %copy-start.2 = (f32[35,35]{1,0:T(8,128)S(1)}, f32[35,35]{1,0:T(8,128)}, u32[]{:S(2)}) copy-start(f32[35,35]{1,0:T(8,128)} %param.18) | copy-start | bytes 14704
  97.9 4.5 %copy-start.3 = (f32[35]{0:T(128)S(1)}, f32[35]{0:T(128)}, u32[]{:S(2)}) copy-start(f32[35]{0:T(128)} %param.17) | copy-start | bytes 424
  98.0 4.5 %copy-start.4 = (f32[3]{0:T(128)S(1)}, f32[3]{0:T(128)}, u32[]{:S(2)}) copy-start(f32[3]{0:T(128)} %param.16) | copy-start | bytes 40
  106.5 7.9 %slice-start.5 = ((s8[10485760]{0:T(1024)(128)(4,1)}), s8[4194304]{0:T(1024)(128)(4,1)S(1)}, s32[]{:S(2)}) async-start(s8[10485760]{0:T(1024)(128)(4,1)} %bitcast.163), calls=%async_computation.6 | async-start | bytes 8388608 | tf_op jit(solution)/shard_map/while
  106.5 7.9 %slice-start.6 = ((s8[10485760]{0:T(1024)(128)(4,1)}), s8[4194304]{0:T(1024)(128)(4,1)S(1)}, s32[]{:S(2)}) async-start(s8[10485760]{0:T(1024)(128)(4,1)} %bitcast.163), calls=%async_computation.7 | async-start | bytes 8388608 | tf_op jit(solution)/shard_map/while
  147.2 7.9 %slice-start.5 = ((s8[10485760]{0:T(1024)(128)(4,1)}), s8[4194304]{0:T(1024)(128)(4,1)S(1)}, s32[]{:S(2)}) async-start(s8[10485760]{0:T(1024)(128)(4,1)} %bitcast.163), calls=%async_computation.6 | async-start | bytes 8388608 | tf_op jit(solution)/shard_map/while
  147.2 7.9 %slice-start.6 = ((s8[10485760]{0:T(1024)(128)(4,1)}), s8[4194304]{0:T(1024)(128)(4,1)S(1)}, s32[]{:S(2)}) async-start(s8[10485760]{0:T(1024)(128)(4,1)} %bitcast.163), calls=%async_computation.7 | async-start | bytes 8388608 | tf_op jit(solution)/shard_map/while
  184.0 24.9 %copy-start.10 = (u32[32]{0:T(128)S(1)}, u32[32]{0:T(128)}, u32[]{:S(2)}) copy-start(u32[32]{0:T(128)} %constant.94) | copy-start | bytes 388
  199.0 10.6 %collective-permute-start.4 = (bf16[2,35,1,32,32]{1,4,3,2,0:T(8,128)(2,1)}, bf16[2,35,1,32,32]{1,4,3,2,0:T(8,128)(2,1)S(1)}, u32[]{:S(2)}, u32[]{:S(2)}) collective-permute-start(bf16[2,35,1,32,32]{1,4,3,2,0:T(8,128)(2,1)} %get-tuple-element.336), channel_id=1, source_target_pairs={{0,1},{1,2},{2,3},{4,5},{5,6},{6,7},{8,9},{9,10},{10,11},{12,13},{... | collective-permute-start | bytes 430088 | tf_op jit(solution)/shard_map/ppermute | solution.py:17
  207.7 3.8 collective-permute-start.5
  229.8 7.8 %slice-start.2 = ((s8[10485760]{0:T(1024)(128)(4,1)}), s8[4194304]{0:T(1024)(128)(4,1)S(1)}, s32[]{:S(2)}) async-start(s8[10485760]{0:T(1024)(128)(4,1)} %bitcast.161), calls=%async_computation.3 | async-start | bytes 8388608 | tf_op jit(solution)/shard_map/while
  229.8 7.8 %slice-start.3 = ((s8[10485760]{0:T(1024)(128)(4,1)}), s8[4194304]{0:T(1024)(128)(4,1)S(1)}, s32[]{:S(2)}) async-start(s8[10485760]{0:T(1024)(128)(4,1)} %bitcast.161), calls=%async_computation.4 | async-start | bytes 8388608 | tf_op jit(solution)/shard_map/while
  237.6 4.7 %slice-start = ((s8[8388608]{0:T(1024)(128)(4,1)}), s8[4194304]{0:T(1024)(128)(4,1)S(1)}, s32[]{:S(2)}) async-start(s8[8388608]{0:T(1024)(128)(4,1)} %bitcast.158), calls=%async_computation.1 | async-start | bytes 8388608 | tf_op jit(solution)/shard_map/while
  268.7 7.8 %slice-start.2 = ((s8[10485760]{0:T(1024)(128)(4,1)}), s8[4194304]{0:T(1024)(128)(4,1)S(1)}, s32[]{:S(2)}) async-start(s8[10485760]{0:T(1024)(128)(4,1)} %bitcast.161), calls=%async_computation.3 | async-start | bytes 8388608 | tf_op jit(solution)/shard_map/while
  268.7 7.8 %slice-start.3 = ((s8[10485760]{0:T(1024)(128)(4,1)}), s8[4194304]{0:T(1024)(128)(4,1)S(1)}, s32[]{:S(2)}) async-start(s8[10485760]{0:T(1024)(128)(4,1)} %bitcast.161), calls=%async_computation.4 | async-start | bytes 8388608 | tf_op jit(solution)/shard_map/while
  276.5 4.7 %slice-start = ((s8[8388608]{0:T(1024)(128)(4,1)}), s8[4194304]{0:T(1024)(128)(4,1)S(1)}, s32[]{:S(2)}) async-start(s8[8388608]{0:T(1024)(128)(4,1)} %bitcast.158), calls=%async_computation.1 | async-start | bytes 8388608 | tf_op jit(solution)/shard_map/while
  319.0 64.4 %copy-start.6 = (f32[1,35,256]{2,0,1:T(1,128)S(1)}, f32[1,35,256]{2,0,1:T(1,128)}, u32[]{:S(2)}) copy-start(f32[1,35,256]{2,0,1:T(1,128)} %param.14) | copy-start | bytes 107524
  (10 other events, 29.1 us)
Sparse Core Ops, SparseCore 0:
  305.8 77.5 all-reduce.2
where the time goes:
time: 394 us; the launch traced here: 393 us
  other arithmetic  110 us (28%)
  local copies, waits for them, and re-layouts  90.3 us (23%)
  waiting for transfers between devices  65.2 us (17%)
  matrix products  58.5 us (15%)
  blocking collectives  33.6 us (9%)
  starting transfers between devices  19.3 us (5%)
  between operations  14.4 us (4%)
    unnamed x2, waiting for transfers between devices  57.2 us
    dot_general x4, matrix products, tendency(): jnp.einsum('fg,...gzyx->...fzyx', stoich, reaction_rate, precision=highest)  56.3 us
    sub x12, other arithmetic, face_flux(): speed * (left_side + right_side) * 0.5 - diffuse * (right_side - left_side)  46.7 us
    all_gather x1, blocking collectives, shards(): lax.all_gather(coarse_send, 'gx', axis=0, tiled=True)  33.6 us
    convert_element_type x2, other arithmetic, extend_layers(): cells.astype(jnp.bfloat16)  17.4 us
    ppermute x3, starting transfers between devices, padded(): lax.ppermute(lax.slice_in_dim(block, block.shape[dim] - width, None, axis...  15.4 us
    concatenate x2, other arithmetic, extend_layers(): return jnp.concatenate([lower_ghost, cells, upper_ghost], 2)  15.1 us
    squeeze x8, local copies, waits for them, and re-layouts, tendency_slots(): return lax.map(tendency_one_slot, (padded_layers, cells))  14.1 us
  transfers between devices with their start and end apart: 7, of which 5 were waited for; matrix products, arithmetic and copies ran while one was open for 5% of the time, Pallas kernels for 0%

commit v1 on v0

--- a/solution.py
+++ b/solution.py
@@ -131,12 +131,19 @@
     layers = layer_cells // (block_edge * block_edge)
     my_slots = owner_group * own_slots + jnp.arange(own_slots, dtype=jnp.int32)
     chooser = (my_slots[:, None] == patch_owner[None, :]).astype(jnp.bfloat16)
-    gathered = jnp.einsum(
-        "oq,qfc->ofc",
-        chooser,
-        lax.all_gather(coarse_send, "gx", axis=0, tiled=True),
-        preferred_element_type=jnp.float32,
-    )
+    size, index, span = (lax.axis_size("gx"), lax.axis_index("gx"), coarse_send.shape[0])
+    ahead = [(i_2, (i_2 + 1) % size) for i_2 in range(size)]
+    held, gathered = (coarse_send, None)
+    for step in range(size):
+        coming = lax.ppermute(held, "gx", ahead) if step < size - 1 else None
+        take_in = jnp.einsum(
+            "oq,qfc->ofc",
+            lax.dynamic_slice_in_dim(chooser, (index - step) % size * span, held.shape[0], axis=1),
+            held,
+            preferred_element_type=jnp.float32,
+        )
+        gathered = take_in if gathered is None else gathered + take_in
+        held = coming
     coarse = gathered.reshape(own_slots, fields, layers, block_edge, block_edge)
     rimmed = padded(coarse.astype(jnp.bfloat16), (("gy", 2),), 1).astype(coarse.dtype)
     below = rimmed[:, :, :-2]

time: 394 us -> 412 us (1.046)
  waiting for transfers between devices: 65.2 us -> 106 us
  blocking collectives: 33.6 us -> 0 us
  local copies, waits for them, and re-layouts: 90.3 us -> 94.9 us
    ppermute x0 -> x7, waiting for transfers between devices: none -> 43.3 us  [shards(): coming = lax.ppermute(held, 'gx', ahead) if step < size - 1 else None]
    all_gather x1 -> x0, blocking collectives: 33.6 us -> none  [shards(): lax.all_gather(coarse_send, 'gx', axis=0, tiled=True)]
    another operation x11 -> x19, local copies, waits for them, and re-layouts: 13.4 us -> 18.3 us
  transfers between devices with their start and end apart: 7 -> 14, of which waited for: 5 -> 11; matrix products, arithmetic and copies ran while one was open for 5% -> 7% of each run, Pallas kernels for 0% -> 0%
where the time goes in v1:
time: 412 us; the launch traced here: 411 us
  other arithmetic  114 us (28%)
  waiting for transfers between devices  106 us (26%)
  local copies, waits for them, and re-layouts  94.9 us (23%)
  matrix products  57.3 us (14%)
  starting transfers between devices  22.6 us (5%)
  between operations  14.5 us (4%)
    dot_general x4, matrix products, tendency(): jnp.einsum('fg,...gzyx->...fzyx', stoich, reaction_rate, precision=highest)  56.2 us
    unnamed x2, waiting for transfers between devices  53.8 us
    sub x12, other arithmetic, face_flux(): speed * (left_side + right_side) * 0.5 - diffuse * (right_side - left_side)  46.8 us
    ppermute x7, waiting for transfers between devices, shards(): coming = lax.ppermute(held, 'gx', ahead) if step < size - 1 else None  43.3 us
    another operation x19, local copies, waits for them, and re-layouts  18.3 us
    convert_element_type x2, other arithmetic, extend_layers(): cells.astype(jnp.bfloat16)  17.5 us
    ppermute x3, starting transfers between devices, padded(): lax.ppermute(lax.slice_in_dim(block, block.shape[dim] - width, None, axis...  15.7 us
    concatenate x2, other arithmetic, extend_layers(): return jnp.concatenate([lower_ghost, cells, upper_ghost], 2)  15.1 us
  transfers between devices with their start and end apart: 14, of which 11 were waited for; matrix products, arithmetic and copies ran while one was open for 7% of the time, Pallas kernels for 0%

profile of v1, /device:TPU:0, one launch (start us, length us, event | category | flops | bytes accessed | tf_op | source)
XLA Modules:
  0.0 410.7 jit_solution(10964056232836558018)
XLA Ops:
  16.2 6.9 %collective-permute-done.1 = bf16[1,35,1024]{2,1,0:T(8,128)(2,1)S(1)} collective-permute-done((bf16[1,35,1024]{2,1,0:T(8,128)(2,1)S(1)}, bf16[1,35,1024]{2,1,0:T(8,128)(2,1)S(1)}, u32[]{:S(2)}, u32[]{:S(2)}) %collective-permute-start.1) | collective-permute-done | bytes 71712 | tf_op jit(solution)/shard_map/ppermute | solution.py:138
  23.3 6.9 %collective-permute-done.2 = bf16[1,35,1024]{2,1,0:T(8,128)(2,1)S(1)} collective-permute-done((bf16[1,35,1024]{2,1,0:T(8,128)(2,1)S(1)}, bf16[1,35,1024]{2,1,0:T(8,128)(2,1)S(1)}, u32[]{:S(2)}, u32[]{:S(2)}) %collective-permute-start.2) | collective-permute-done | bytes 71712 | tf_op jit(solution)/shard_map/ppermute | solution.py:138
  30.5 6.9 %collective-permute-done.3 = bf16[1,35,1024]{2,1,0:T(8,128)(2,1)S(1)} collective-permute-done((bf16[1,35,1024]{2,1,0:T(8,128)(2,1)S(1)}, bf16[1,35,1024]{2,1,0:T(8,128)(2,1)S(1)}, u32[]{:S(2)}, u32[]{:S(2)}) %collective-permute-start.3) | collective-permute-done | bytes 71712 | tf_op jit(solution)/shard_map/ppermute | solution.py:138
  38.4 6.1 %collective-permute-done.4 = bf16[1,35,1024]{2,1,0:T(8,128)(2,1)S(1)} collective-permute-done((bf16[1,35,1024]{2,1,0:T(8,128)(2,1)S(1)}, bf16[1,35,1024]{2,1,0:T(8,128)(2,1)S(1)}, u32[]{:S(2)}, u32[]{:S(2)}) %collective-permute-start.4) | collective-permute-done | bytes 71712 | tf_op jit(solution)/shard_map/ppermute | solution.py:138
  45.6 6.6 %collective-permute-done.5 = bf16[1,35,1024]{2,1,0:T(8,128)(2,1)S(1)} collective-permute-done((bf16[1,35,1024]{2,1,0:T(8,128)(2,1)S(1)}, bf16[1,35,1024]{2,1,0:T(8,128)(2,1)S(1)}, u32[]{:S(2)}, u32[]{:S(2)}) %collective-permute-start.5) | collective-permute-done | bytes 71712 | tf_op jit(solution)/shard_map/ppermute | solution.py:138
  53.3 6.1 %collective-permute-done.6 = bf16[1,35,1024]{2,1,0:T(8,128)(2,1)S(1)} collective-permute-done((bf16[1,35,1024]{2,1,0:T(8,128)(2,1)S(1)}, bf16[1,35,1024]{2,1,0:T(8,128)(2,1)S(1)}, u32[]{:S(2)}, u32[]{:S(2)}) %collective-permute-start.6) | collective-permute-done | bytes 71712 | tf_op jit(solution)/shard_map/ppermute | solution.py:138
  74.1 17.1 %while.49 = (s32[]{:T(128)}, f32[2,35,8,32,32]{1,4,3,2,0:T(8,128)}, f32[2,35,4,16,16]{1,4,3,2,0:T(8,128)S(1)}, f32[2,35,4,16,16]{1,4,3,2,0:T(8,128)S(1)}, s32[]{:T(128)}, /*index=5*/f32[2]{0:T(128)S(1)}) while((s32[]{:T(128)}, f32[2,35,8,32,32]{1,4,3,2,0:T(8,128)}, f32[2,35,4,16,16]{1,4,3,2,0:T(8,128)S(1)}, ...), condition=%wide.region_1.2_spmd.clone, body=%wide.region_0.1_spmd.sunk.clone.sunk | while | flops 1496322 | bytes 12653153 | solution.py:91
  91.2 4.5 %convert_element_type.22 = bf16[2,35,8,32,32]{1,4,3,2,0:T(8,128)(2,1)S(1)} convert(f32[2,35,8,32,32]{1,4,3,2,0:T(8,128)} %get-tuple-element.593) | non-fusion elementwise | flops 573440 | bytes 3440640 | tf_op jit(solution)/shard_map/convert_element_type | solution.py:162
  99.1 6.1 %collective-permute-start.9 = (bf16[2,35,1,32,32]{1,4,3,2,0:T(8,128)(2,1)S(1)}, bf16[2,35,1,32,32]{1,4,3,2,0:T(8,128)(2,1)S(1)}, u32[]{:S(2)}, u32[]{:S(2)}) collective-permute-start(bf16[2,35,1,32,32]{1,4,3,2,0:T(8,128)(2,1)S(1)} %get-tuple-element.334), channel_id=1, source_target_pairs={{0,1},{1,2},{2,3},{4,5},{5,6},{6,7},{8,9},{9,10},{10,11},{12,13},{... | collective-permute-start | bytes 430088 | tf_op jit(solution)/shard_map/ppermute | solution.py:17
  108.6 9.3 %pad_maximum_fusion.8 = f32[2,35,10,32,32]{1,4,3,2,0:T(8,128)} fusion(f32[2,35,1,32,32]{1,4,3,2,0:T(8,128)S(1)} %get-tuple-element.331, f32[2,35,8,32,32]{1,4,3,2,0:T(8,128)} %get-tuple-element.593, f32[2,35,1,32,32]{1,4,3,2,0:T(8,128)S(1)} %get-tuple-element.330), kind=kLoop, calls=%fused_computation.78 | loop fusion | flops 1433600 | bytes 5734400 | tf_op jit(solution)/shard_map/concatenate | solution.py:165
  122.4 81.4 %while.47 = (s32[]{:T(128)}, f32[2,35,8,32,32]{1,4,3,2,0:T(8,128)}, f32[2,35,8,32]{1,3,2,0:T(8,128)S(1)}, f32[2,35,8,32]{1,3,2,0:T(8,128)S(1)}, f32[2,35,8,32]{1...) while((s32[]{:T(128)}, f32[2,35,8,32,32]{1,4,3,2,0:T(8,128)}, ...), condition=%wide.region_3.4_spmd, body=%wide.region_2.3_spmd.sunk | while | flops 129128448 | bytes 80370104 | solution.py:82
  138.5 4.6 %constant_dynamic-slice_fusion.12 = f32[1,1,8,32,32]{1,4,3,2,0:T(8,128)} fusion(f32[2,35,8,32,32]{1,4,3,2,0:T(8,128)} %get-tuple-element.617, s32[]{:T(128)} %get-tuple-element.599), kind=kLoop, calls=%fused_computation.26.clone.1 | loop fusion | bytes 65540 | tf_op jit(solution)/shard_map/while/body/eval_jaxpr/slice | solution.py:66
  146.4 14.0 %fusion.88 = f32[2,35,8,32,32]{1,4,3,2,0:T(8,128)} fusion(f32[2,35,8,32,32]{1,4,3,2,0:T(8,128)} %get-tuple-element.600, s32[]{:T(128)} %get-tuple-element.599, f32[35,9,32,32]{0,3,2,1:T(8,128)} %multiply_subtract_fusion.12, f32[35,8,33,32]{0,3,2,1:T(8,128)} %multiply_subtract_fusion.13, f32[35,8,32,33]{0,3,2,1:T(8,128)} %multiply_subtract_fusion.14, ...), kind=kOutput, calls=%fused_computation.12.clone.1 | convolution fusion | flops 122429440 | bytes 33593124 | tf_op jit(solution)/shard_map/while/body/eval_jaxpr/fg,...gzyx->...fzyx/dot_general | solution.py:67
  179.2 4.6 %constant_dynamic-slice_fusion.12 = f32[1,1,8,32,32]{1,4,3,2,0:T(8,128)} fusion(f32[2,35,8,32,32]{1,4,3,2,0:T(8,128)} %get-tuple-element.617, s32[]{:T(128)} %get-tuple-element.599), kind=kLoop, calls=%fused_computation.26.clone.1 | loop fusion | bytes 65540 | tf_op jit(solution)/shard_map/while/body/eval_jaxpr/slice | solution.py:66
  187.0 14.1 %fusion.88 = f32[2,35,8,32,32]{1,4,3,2,0:T(8,128)} fusion(f32[2,35,8,32,32]{1,4,3,2,0:T(8,128)} %get-tuple-element.600, s32[]{:T(128)} %get-tuple-element.599, f32[35,9,32,32]{0,3,2,1:T(8,128)} %multiply_subtract_fusion.12, f32[35,8,33,32]{0,3,2,1:T(8,128)} %multiply_subtract_fusion.13, f32[35,8,32,33]{0,3,2,1:T(8,128)} %multiply_subtract_fusion.14, ...), kind=kOutput, calls=%fused_computation.12.clone.1 | convolution fusion | flops 122429440 | bytes 33593124 | tf_op jit(solution)/shard_map/while/body/eval_jaxpr/fg,...gzyx->...fzyx/dot_general | solution.py:67
  203.8 12.9 %fusion.52 = (bf16[2,35,8,32,32]{1,4,3,2,0:T(8,128)(2,1)}, f32[2,35,8,32,32]{1,4,3,2,0:T(8,128)}) fusion(f32[2,35,8,32,32]{1,4,3,2,0:T(8,128)} %get-tuple-element.593, f32[2,35,8,32,32]{1,4,3,2,0:T(8,128)} %get-tuple-element.152), kind=kLoop, calls=%fused_computation.148 | loop fusion | flops 1720320 | bytes 8028160 | tf_op jit(solution)/shard_map/convert_element_type | solution.py:162
  218.9 8.2 %collective-permute-start.11 = (bf16[2,35,1,32,32]{1,4,3,2,0:T(8,128)(2,1)}, bf16[2,35,1,32,32]{1,4,3,2,0:T(8,128)(2,1)S(1)}, u32[]{:S(2)}, u32[]{:S(2)}) collective-permute-start(bf16[2,35,1,32,32]{1,4,3,2,0:T(8,128)(2,1)} %get-tuple-element.332), channel_id=1, source_target_pairs={{0,1},{1,2},{2,3},{4,5},{5,6},{6,7},{8,9},{9,10},{10,11},{12,13},{... | collective-permute-start | bytes 430088 | tf_op jit(solution)/shard_map/ppermute | solution.py:17
  236.9 5.8 %pad_maximum_fusion.9 = f32[2,35,10,32,32]{1,4,3,2,0:T(8,128)} fusion(f32[2,35,1,32,32]{1,4,3,2,0:T(8,128)S(1)} %get-tuple-element.329, f32[2,35,8,32,32]{1,4,3,2,0:T(8,128)S(1)} %copy-done, f32[2,35,1,32,32]{1,4,3,2,0:T(8,128)S(1)} %get-tuple-element.328), kind=kLoop, calls=%fused_computation.79 | loop fusion | flops 1433600 | bytes 5734400 | tf_op jit(solution)/shard_map/concatenate | solution.py:165
  247.2 78.4 %while.48 = (s32[]{:T(128)}, f32[2,35,8,32,32]{1,4,3,2,0:T(8,128)}, f32[2,35,8,32]{1,3,2,0:T(8,128)S(1)}, f32[2,35,8,32]{1,3,2,0:T(8,128)S(1)}, f32[2,35,8,32]{1...) while((s32[]{:T(128)}, f32[2,35,8,32,32]{1,4,3,2,0:T(8,128)}, ...), condition=%wide.region_5.6_spmd, body=%wide.region_4.5_spmd.sunk | while | flops 129128448 | bytes 105535960 | solution.py:82
  269.7 14.1 %fusion.96 = f32[2,35,8,32,32]{1,4,3,2,0:T(8,128)} fusion(f32[2,35,8,32,32]{1,4,3,2,0:T(8,128)} %get-tuple-element.636, s32[]{:T(128)} %get-tuple-element.635, f32[35,9,32,32]{0,3,2,1:T(8,128)} %multiply_subtract_fusion.15, f32[35,8,33,32]{0,3,2,1:T(8,128)} %multiply_subtract_fusion.16, f32[35,8,32,33]{0,3,2,1:T(8,128)} %multiply_subtract_fusion.17, ...), kind=kOutput, calls=%fused_computation.41.clone.1 | convolution fusion | flops 122429440 | bytes 33593124 | tf_op jit(solution)/shard_map/while/body/eval_jaxpr/fg,...gzyx->...fzyx/dot_general | solution.py:67
  308.8 14.1 %fusion.96 = f32[2,35,8,32,32]{1,4,3,2,0:T(8,128)} fusion(f32[2,35,8,32,32]{1,4,3,2,0:T(8,128)} %get-tuple-element.636, s32[]{:T(128)} %get-tuple-element.635, f32[35,9,32,32]{0,3,2,1:T(8,128)} %multiply_subtract_fusion.15, f32[35,8,33,32]{0,3,2,1:T(8,128)} %multiply_subtract_fusion.16, f32[35,8,32,33]{0,3,2,1:T(8,128)} %multiply_subtract_fusion.17, ...), kind=kOutput, calls=%fused_computation.41.clone.1 | convolution fusion | flops 122429440 | bytes 33593124 | tf_op jit(solution)/shard_map/while/body/eval_jaxpr/fg,...gzyx->...fzyx/dot_general | solution.py:67
  327.4 13.4 %multiply_add_fusion.1 = f32[2,35,8,32,32]{1,4,3,2,0:T(8,128)} fusion(f32[2,35,8,32,32]{1,4,3,2,0:T(8,128)} %get-tuple-element.593, f32[2,35,8,32,32]{1,4,3,2,0:T(8,128)} %get-tuple-element.152, f32[2,35,8,32,32]{1,4,3,2,0:T(8,128)} %get-tuple-element.153), kind=kLoop, calls=%fused_computation.80 | loop fusion | flops 1720320 | bytes 9175040 | tf_op jit(solution)/shard_map/add | solution.py:174
  340.7 7.2 %copy.68 = f32[2,35,8192]{2,0,1:T(2,128)} copy(f32[2,35,8192]{1,2,0:T(8,128)} %bitcast.204) | data formatting | bytes 4587520 | tf_op jit(solution)/shard_map/reshape | solution.py:182
  348.0 53.7 %all-reduce.3.cloned.1.call-done = f32[8,35,256]{2,0,1:T(8,128)} async-done(((f32[8,35,256]{2,0,1:T(8,128)}), f32[8,35,256]{2,0,1:T(8,128)}) %all-reduce.3.cloned.1.call-update) | async-done | bytes 286736
  (217 shorter events, 169.0 us)
Async XLA Ops:
  7.2 394.5 %all-reduce.3.cloned.1.call-start = ((), (), s32[]{:S(2)}) async-start(), calls=%async_computation | async-start | bytes 573440
  7.2 8.7 %collective-permute-start = (bf16[1,35,1024]{2,1,0:T(8,128)(2,1)}, bf16[1,35,1024]{2,1,0:T(8,128)(2,1)S(1)}, u32[]{:S(2)}, u32[]{:S(2)}) collective-permute-start(bf16[1,35,1024]{2,1,0:T(8,128)(2,1)} %param.13), channel_id=1, source_target_pairs={{0,4},{4,8},{8,12},{12,16},{16,20},{20,24},{24,28},{28,0},{1,5},{5... | collective-permute-start | bytes 215048 | tf_op jit(solution)/shard_map/ppermute | solution.py:138
  15.9 7.1 %collective-permute-start.1 = (bf16[1,35,1024]{2,1,0:T(8,128)(2,1)S(1)}, bf16[1,35,1024]{2,1,0:T(8,128)(2,1)S(1)}, u32[]{:S(2)}, u32[]{:S(2)}) collective-permute-start(bf16[1,35,1024]{2,1,0:T(8,128)(2,1)S(1)} %collective-permute-done), channel_id=1, source_target_pairs={{0,4},{4,8},{8,12},{12,16},{16,20},{20,24},{24,28},{28,0},{1,5},{5... | collective-permute-start | bytes 215048 | tf_op jit(solution)/shard_map/ppermute | solution.py:138
  23.1 7.1 %collective-permute-start.2 = (bf16[1,35,1024]{2,1,0:T(8,128)(2,1)S(1)}, bf16[1,35,1024]{2,1,0:T(8,128)(2,1)S(1)}, u32[]{:S(2)}, u32[]{:S(2)}) collective-permute-start(bf16[1,35,1024]{2,1,0:T(8,128)(2,1)S(1)} %collective-permute-done.1), channel_id=1, source_target_pairs={{0,4},{4,8},{8,12},{12,16},{16,20},{20,24},{24,28},{28,0},{1,5},{5... | collective-permute-start | bytes 215048 | tf_op jit(solution)/shard_map/ppermute | solution.py:138
  30.2 7.1 %collective-permute-start.3 = (bf16[1,35,1024]{2,1,0:T(8,128)(2,1)S(1)}, bf16[1,35,1024]{2,1,0:T(8,128)(2,1)S(1)}, u32[]{:S(2)}, u32[]{:S(2)}) collective-permute-start(bf16[1,35,1024]{2,1,0:T(8,128)(2,1)S(1)} %collective-permute-done.2), channel_id=1, source_target_pairs={{0,4},{4,8},{8,12},{12,16},{16,20},{20,24},{24,28},{28,0},{1,5},{5... | collective-permute-start | bytes 215048 | tf_op jit(solution)/shard_map/ppermute | solution.py:138
  37.4 7.2 %collective-permute-start.4 = (bf16[1,35,1024]{2,1,0:T(8,128)(2,1)S(1)}, bf16[1,35,1024]{2,1,0:T(8,128)(2,1)S(1)}, u32[]{:S(2)}, u32[]{:S(2)}) collective-permute-start(bf16[1,35,1024]{2,1,0:T(8,128)(2,1)S(1)} %collective-permute-done.3), channel_id=1, source_target_pairs={{0,4},{4,8},{8,12},{12,16},{16,20},{20,24},{24,28},{28,0},{1,5},{5... | collective-permute-start | bytes 215048 | tf_op jit(solution)/shard_map/ppermute | solution.py:138
  44.5 7.7 %collective-permute-start.5 = (bf16[1,35,1024]{2,1,0:T(8,128)(2,1)S(1)}, bf16[1,35,1024]{2,1,0:T(8,128)(2,1)S(1)}, u32[]{:S(2)}, u32[]{:S(2)}) collective-permute-start(bf16[1,35,1024]{2,1,0:T(8,128)(2,1)S(1)} %collective-permute-done.4), channel_id=1, source_target_pairs={{0,4},{4,8},{8,12},{12,16},{16,20},{20,24},{24,28},{28,0},{1,5},{5... | collective-permute-start | bytes 215048 | tf_op jit(solution)/shard_map/ppermute | solution.py:138
  52.2 7.1 %collective-permute-start.6 = (bf16[1,35,1024]{2,1,0:T(8,128)(2,1)S(1)}, bf16[1,35,1024]{2,1,0:T(8,128)(2,1)S(1)}, u32[]{:S(2)}, u32[]{:S(2)}) collective-permute-start(bf16[1,35,1024]{2,1,0:T(8,128)(2,1)S(1)} %collective-permute-done.5), channel_id=1, source_target_pairs={{0,4},{4,8},{8,12},{12,16},{16,20},{20,24},{24,28},{28,0},{1,5},{5... | collective-permute-start | bytes 215048 | tf_op jit(solution)/shard_map/ppermute | solution.py:138
  62.6 2.6 collective-permute-start.7
  63.9 5.1 %collective-permute-start.8 = (bf16[2,35,1,16,16]{1,4,3,2,0:T(8,128)(2,1)S(1)}, bf16[2,35,1,16,16]{1,4,3,2,0:T(8,128)(2,1)S(1)}, u32[]{:S(2)}, u32[]{:S(2)}) collective-permute-start(bf16[2,35,1,16,16]{1,4,3,2,0:T(8,128)(2,1)S(1)} %get-tuple-element.337), channel_id=1, source_target_pairs={{1,0},{2,1},{3,2},{5,4},{6,5},{7,6},{9,8},{10,9},{11,10},{13,12},{... | collective-permute-start | bytes 107528 | tf_op jit(solution)/shard_map/ppermute | solution.py:20
  97.8 7.4 %collective-permute-start.10 = (bf16[2,35,1,32,32]{1,4,3,2,0:T(8,128)(2,1)S(1)}, bf16[2,35,1,32,32]{1,4,3,2,0:T(8,128)(2,1)S(1)}, u32[]{:S(2)}, u32[]{:S(2)}) collective-permute-start(bf16[2,35,1,32,32]{1,4,3,2,0:T(8,128)(2,1)S(1)} %get-tuple-element.335), channel_id=1, source_target_pairs={{1,0},{2,1},{3,2},{5,4},{6,5},{7,6},{9,8},{10,9},{11,10},{13,12},{... | collective-permute-start | bytes 430088 | tf_op jit(solution)/shard_map/ppermute | solution.py:20
  99.1 7.6 %collective-permute-start.9 = (bf16[2,35,1,32,32]{1,4,3,2,0:T(8,128)(2,1)S(1)}, bf16[2,35,1,32,32]{1,4,3,2,0:T(8,128)(2,1)S(1)}, u32[]{:S(2)}, u32[]{:S(2)}) collective-permute-start(bf16[2,35,1,32,32]{1,4,3,2,0:T(8,128)(2,1)S(1)} %get-tuple-element.334), channel_id=1, source_target_pairs={{0,1},{1,2},{2,3},{4,5},{5,6},{6,7},{8,9},{9,10},{10,11},{12,13},{... | collective-permute-start | bytes 430088 | tf_op jit(solution)/shard_map/ppermute | solution.py:17
  126.4 7.8 %slice-start.5 = ((s8[10485760]{0:T(1024)(128)(4,1)}), s8[4194304]{0:T(1024)(128)(4,1)S(1)}, s32[]{:S(2)}) async-start(s8[10485760]{0:T(1024)(128)(4,1)} %bitcast.200), calls=%async_computation.6 | async-start | bytes 8388608 | tf_op jit(solution)/shard_map/while
  126.4 7.8 %slice-start.6 = ((s8[10485760]{0:T(1024)(128)(4,1)}), s8[4194304]{0:T(1024)(128)(4,1)S(1)}, s32[]{:S(2)}) async-start(s8[10485760]{0:T(1024)(128)(4,1)} %bitcast.200), calls=%async_computation.7 | async-start | bytes 8388608 | tf_op jit(solution)/shard_map/while
  167.0 7.8 %slice-start.5 = ((s8[10485760]{0:T(1024)(128)(4,1)}), s8[4194304]{0:T(1024)(128)(4,1)S(1)}, s32[]{:S(2)}) async-start(s8[10485760]{0:T(1024)(128)(4,1)} %bitcast.200), calls=%async_computation.6 | async-start | bytes 8388608 | tf_op jit(solution)/shard_map/while
  167.0 7.8 %slice-start.6 = ((s8[10485760]{0:T(1024)(128)(4,1)}), s8[4194304]{0:T(1024)(128)(4,1)S(1)}, s32[]{:S(2)}) async-start(s8[10485760]{0:T(1024)(128)(4,1)} %bitcast.200), calls=%async_computation.7 | async-start | bytes 8388608 | tf_op jit(solution)/shard_map/while
  203.8 24.6 %copy-start.10 = (u32[32]{0:T(128)S(1)}, u32[32]{0:T(128)}, u32[]{:S(2)}) copy-start(u32[32]{0:T(128)} %constant.152) | copy-start | bytes 388
  218.9 10.2 %collective-permute-start.11 = (bf16[2,35,1,32,32]{1,4,3,2,0:T(8,128)(2,1)}, bf16[2,35,1,32,32]{1,4,3,2,0:T(8,128)(2,1)S(1)}, u32[]{:S(2)}, u32[]{:S(2)}) collective-permute-start(bf16[2,35,1,32,32]{1,4,3,2,0:T(8,128)(2,1)} %get-tuple-element.332), channel_id=1, source_target_pairs={{0,1},{1,2},{2,3},{4,5},{5,6},{6,7},{8,9},{9,10},{10,11},{12,13},{... | collective-permute-start | bytes 430088 | tf_op jit(solution)/shard_map/ppermute | solution.py:17
  227.1 5.8 %collective-permute-start.12 = (bf16[2,35,1,32,32]{1,4,3,2,0:T(8,128)(2,1)S(1)}, bf16[2,35,1,32,32]{1,4,3,2,0:T(8,128)(2,1)S(1)}, u32[]{:S(2)}, u32[]{:S(2)}) collective-permute-start(bf16[2,35,1,32,32]{1,4,3,2,0:T(8,128)(2,1)S(1)} %get-tuple-element.333), channel_id=1, source_target_pairs={{1,0},{2,1},{3,2},{5,4},{6,5},{7,6},{9,8},{10,9},{11,10},{13,12},{... | collective-permute-start | bytes 430088 | tf_op jit(solution)/shard_map/ppermute | solution.py:20
  251.3 8.0 %slice-start.2 = ((s8[10485760]{0:T(1024)(128)(4,1)}), s8[4194304]{0:T(1024)(128)(4,1)S(1)}, s32[]{:S(2)}) async-start(s8[10485760]{0:T(1024)(128)(4,1)} %bitcast.198), calls=%async_computation.3 | async-start | bytes 8388608 | tf_op jit(solution)/shard_map/while
  251.3 8.0 %slice-start.3 = ((s8[10485760]{0:T(1024)(128)(4,1)}), s8[4194304]{0:T(1024)(128)(4,1)S(1)}, s32[]{:S(2)}) async-start(s8[10485760]{0:T(1024)(128)(4,1)} %bitcast.198), calls=%async_computation.4 | async-start | bytes 8388608 | tf_op jit(solution)/shard_map/while
  290.4 8.0 %slice-start.2 = ((s8[10485760]{0:T(1024)(128)(4,1)}), s8[4194304]{0:T(1024)(128)(4,1)S(1)}, s32[]{:S(2)}) async-start(s8[10485760]{0:T(1024)(128)(4,1)} %bitcast.198), calls=%async_computation.3 | async-start | bytes 8388608 | tf_op jit(solution)/shard_map/while
  290.4 8.0 %slice-start.3 = ((s8[10485760]{0:T(1024)(128)(4,1)}), s8[4194304]{0:T(1024)(128)(4,1)S(1)}, s32[]{:S(2)}) async-start(s8[10485760]{0:T(1024)(128)(4,1)} %bitcast.198), calls=%async_computation.4 | async-start | bytes 8388608 | tf_op jit(solution)/shard_map/while
  340.7 61.0 %copy-start.6 = (f32[1,35,256]{2,0,1:T(1,128)S(1)}, f32[1,35,256]{2,0,1:T(1,128)}, u32[]{:S(2)}) copy-start(f32[1,35,256]{2,0,1:T(1,128)} %param.14) | copy-start | bytes 107524
  (17 other events, 57.4 us)
Sparse Core Ops, SparseCore 0:
  327.5 74.1 all-reduce.2
